TPU v7x, 512 devices: a whole 4x8x8 slice. The times are simulated.
512 devices in a mesh: rows: 32 (over x_hi, y, core), snaps: 16 (over z, x_lo).
Axes of the slice: x: 4 (x_hi: 2, x_lo: 2; x = x_hi * 2 + x_lo), y: 8, z: 8, core: 2. Of those that a mesh axis runs over, the one named last changes fastest.
Arguments:
- snapshots: bfloat16 [4096, 32768], P('rows', 'snaps'), may hold values from -6 to 6
- linear_basis: bfloat16 [4096, 64], P(('rows', 'snaps')), may hold values from -0.75 to 0.75
- quad_weights: bfloat16 [4096, 2080], P(('rows', 'snaps')), may hold values from -0.125 to 0.125
- coordinates: bfloat16 [64, 32768], P(None, 'snaps'), may hold values from -5 to 5
Outputs:
- grad_basis: float32 [4096, 64], P(('rows', 'snaps'))
- grad_quad: float32 [4096, 2080], P(('rows', 'snaps'))
- grad_coords: float32 [64, 32768], P('rows', 'snaps')
All inputs are finite; a program needn't handle non-finite values.
Results may differ from a plain program's by a relative error of at most 0.0012.
Values may be sent and summed in bfloat16 or wider, within the bound.
No kernel may reach another device: no remote copies, remote signals or barrier semaphores. Data moves between devices by JAX's collectives and lax.ppermute only.
A program may use at most 64 MiB of HBM per device.

v0:
```python
import math

import jax
import jax.numpy as jnp
import numpy as np
from jax import lax
from jax.sharding import PartitionSpec as P


def pair_tables(count):
    lead_index, tail_index = np.triu_indices(count)
    pair_total = lead_index.shape[0]
    lead_table = np.zeros((pair_total, count), np.float32)
    tail_table = np.zeros((pair_total, count), np.float32)
    lead_table[np.arange(pair_total), lead_index] = 1.0
    tail_table[np.arange(pair_total), tail_index] = 1.0
    return (lead_table, tail_table)


def shards(snapshots, linear_basis, quad_weights, coordinates):
    coord_count = coordinates.shape[0]
    local_rows, snap_dev = snapshots.shape
    high = lax.Precision.HIGHEST
    lead_np, tail_np = pair_tables(coord_count)
    lead_f32 = jnp.asarray(lead_np)
    tail_f32 = jnp.asarray(tail_np)
    lead_bf16 = lead_f32.astype(jnp.bfloat16)
    tail_bf16 = tail_f32.astype(jnp.bfloat16)
    lin_rows, quad_rows = (
        lax.all_gather(linear_basis, "snaps", axis=0, tiled=True),
        lax.all_gather(quad_weights, "snaps", axis=0, tiled=True),
    )
    block_width = min(256, snap_dev)
    block_total = snap_dev // block_width
    contract_rows = (((0,), (0,)), ((), ()))
    contract_cols = (((1,), (1,)), ((), ()))

    def block_core(start_col):
        coord_block = lax.dynamic_slice_in_dim(coordinates, start_col, block_width, 1)
        snap_block = lax.dynamic_slice_in_dim(snapshots, start_col, block_width, 1)
        lead_vals = jnp.dot(lead_bf16, coord_block, preferred_element_type=jnp.float32)
        tail_vals = jnp.dot(tail_bf16, coord_block, preferred_element_type=jnp.float32)
        quad_block = (lead_vals * tail_vals).astype(jnp.bfloat16)
        rebuilt = jnp.dot(lin_rows, coord_block, preferred_element_type=jnp.float32)
        rebuilt = rebuilt + jnp.dot(quad_rows, quad_block, preferred_element_type=jnp.float32)
        residual = (rebuilt - snap_block.astype(jnp.float32)).astype(jnp.bfloat16)
        back_lin = lax.dot_general(
            lin_rows, residual, contract_rows, preferred_element_type=jnp.float32
        )
        back_quad = lax.dot_general(
            quad_rows, residual, contract_rows, preferred_element_type=jnp.float32
        )
        terms = back_lin + lax.dot_general(
            lead_f32, back_quad * tail_vals, contract_rows, precision=high
        )
        terms = terms + lax.dot_general(
            tail_f32, back_quad * lead_vals, contract_rows, precision=high
        )
        return (coord_block, quad_block, residual, terms)

    def block_step(block_index, loop_state):
        lin_grad, quad_grad, coord_part = loop_state
        start_col = block_index * block_width
        coord_block, quad_block, residual, terms = block_core(start_col)
        lin_grad = lin_grad + lax.dot_general(
            residual, coord_block, contract_cols, preferred_element_type=jnp.float32
        )
        quad_grad = quad_grad + lax.dot_general(
            residual, quad_block, contract_cols, preferred_element_type=jnp.float32
        )
        coord_part = lax.dynamic_update_slice_in_dim(coord_part, terms, start_col, 1)
        return (lin_grad, quad_grad, coord_part)

    start_state = (
        jnp.zeros((local_rows, coord_count), jnp.float32),
        jnp.zeros((local_rows, quad_weights.shape[1]), jnp.float32),
        jnp.zeros((coord_count, snap_dev), jnp.float32),
    )
    lin_grad, quad_grad, coord_part = lax.fori_loop(0, block_total, block_step, start_state)
    lin_sum, quad_sum = (
        lax.psum_scatter(lin_grad, "snaps", scatter_dimension=0, tiled=True),
        lax.psum_scatter(quad_grad, "snaps", scatter_dimension=0, tiled=True),
    )
    coord_share = lax.psum_scatter(coord_part, "rows", scatter_dimension=0, tiled=True)
    grad_coords = coord_share * (1.0 / math.sqrt(local_rows * lax.axis_size("rows")))
    model_scale = 1.0 / math.sqrt(snap_dev * lax.axis_size("snaps"))
    return (lin_sum * model_scale, quad_sum * model_scale, grad_coords)


def solution(mesh):
    placed = (
        P("rows", "snaps"),
        P(("rows", "snaps"), None),
        P(("rows", "snaps"), None),
        P(None, "snaps"),
    )
    return jax.shard_map(
        shards,
        mesh=mesh,
        in_specs=placed,
        out_specs=(P(("rows", "snaps"), None), P(("rows", "snaps"), None), P("rows", "snaps")),
        check_vma=False,
    )
```

profile of v0, /device:TPU:4, one launch (start us, length us, event | category | flops | bytes accessed | tf_op | source)
XLA Modules:
  0.0 647.3 jit_solution(6802540742337190230)
XLA Ops:
  7.2 39.7 %all_gather.6 = bf16[128,64]{1,0:T(8,128)(2,1)S(1)} all-gather(bf16[8,64]{1,0:T(8,128)(2,1)} %param.9), channel_id=1, replica_groups=mesh['rows'=32,'snaps'=16] {'snaps'}, dimensions={0}, use_global_device_ids=true | all-gather | bytes 17408 | tf_op jit(solution)/shard_map/all_gather | solution.py:30
  47.0 35.0 %all_gather.7 = bf16[128,2080]{1,0:T(8,128)(2,1)} all-gather(bf16[8,2080]{1,0:T(8,128)(2,1)} %param.10), channel_id=1, replica_groups=mesh['rows'=32,'snaps'=16] {'snaps'}, dimensions={0}, use_global_device_ids=true | all-gather | bytes 565760 | tf_op jit(solution)/shard_map/all_gather | solution.py:31
  82.8 136.3 %while.20 = (s32[]{:T(128)}, f32[128,64]{0,1:T(8,128)S(1)}, f32[128,2080]{0,1:T(8,128)}, f32[64,2048]{1,0:T(8,128)}, bf16[64,2048]{1,0:T(8,128)(2,1)}, /*index=5...) while((s32[]{:T(128)}, f32[128,64]{0,1:T(8,128)S(1)}, ...), condition=%wide.region_1.0_spmd.clone.clone.clone, body=%wide.region_0.0_spmd.sunk.clone.clone.clone.sunk | while | flops 1378574336 | bytes 43540892 | solution.py:79
  85.0 2.5 multiply_convert_fusion.2
  96.0 2.7 fusion.101
  100.9 2.5 multiply_convert_fusion.2
  106.9 2.7 convolution_add_fusion.6
  113.2 2.7 fusion.101
  124.1 2.7 convolution_add_fusion.6
  130.4 2.7 fusion.101
  141.4 2.7 convolution_add_fusion.6
  147.6 2.7 fusion.101
  158.6 2.7 convolution_add_fusion.6
  164.8 2.7 fusion.101
  175.8 2.7 convolution_add_fusion.6
  182.0 2.7 fusion.101
  192.9 2.7 convolution_add_fusion.6
  199.2 2.7 fusion.101
  210.1 2.7 convolution_add_fusion.6
  216.4 2.7 fusion.101
  219.2 2.6 copy.14
  225.8 61.9 %all-reduce = f32[128,64]{1,0:T(8,128)S(1)} all-reduce(f32[128,64]{1,0:T(8,128)S(1)} %copy.13), channel_id=2, replica_groups=mesh['rows'=32,'snaps'=16] {'snaps'}, use_global_device_ids=true, to_apply=%region_2.0.clone | all-reduce | flops 8192 | bytes 65536
  288.3 201.6 %all-reduce.8.cloned.1.call-done = f32[64,2048]{1,0:T(8,128)} async-done(((f32[64,2048]{1,0:T(8,128)}), f32[64,2048]{1,0:T(8,128)}) %all-reduce.8.cloned.1.call-update) | async-done | bytes 524304
  491.4 147.5 %all-reduce.6.cloned.1.call-done = f32[128,2080]{1,0:T(8,128)} async-done(((f32[128,2080]{1,0:T(8,128)}), f32[128,2080]{1,0:T(8,128)}) %all-reduce.6.cloned.1.call-update) | async-done | bytes 1064976
  (190 shorter events, 96.5 us)
Async XLA Ops:
  7.2 75.7 %copy-start.5 = (bf16[2080,64]{1,0:T(8,128)(2,1)S(1)}, bf16[2080,64]{1,0:T(8,128)(2,1)}, u32[]{:S(2)}) copy-start(bf16[2080,64]{1,0:T(8,128)(2,1)} %constant.89) | copy-start | bytes 798724
  7.2 482.8 %all-reduce.8.cloned.1.call-start = ((), (), s32[]{:S(2)}) async-start(), calls=%async_computation.1 | async-start | bytes 1048576
  93.9 2.1 copy-start.3
  96.0 2.7 copy-start.6
  106.9 2.9 copy-start.1
  111.1 2.1 copy-start.3
  113.2 2.7 copy-start.6
  124.1 2.9 copy-start.1
  128.3 2.1 copy-start.3
  130.4 2.8 copy-start.6
  141.3 2.9 copy-start.1
  145.5 2.1 copy-start.3
  147.6 2.7 copy-start.6
  158.5 2.9 copy-start.1
  164.8 2.7 copy-start.6
  175.7 2.9 copy-start.1
  179.9 2.1 copy-start.3
  182.0 2.7 copy-start.6
  192.9 2.9 copy-start.1
  199.2 2.7 copy-start.6
  210.1 2.9 copy-start.1
  214.3 2.1 copy-start.3
  216.4 2.7 copy-start.6
  219.2 419.8 %all-reduce.6.cloned.1.call-start = ((), (), s32[]{:S(2)}) async-start(), calls=%async_computation | async-start | bytes 2228224
  (27 other events, 42.5 us)
Sparse Core Ops, SparseCore 0:
  219.3 270.5 all-reduce.7
  492.9 145.9 all-reduce.5
where the time goes:
time: 651 us; the launch traced here: 647 us
  waiting for transfers between devices  349 us (54%)
  blocking collectives  137 us (21%)
  matrix products  122 us (19%)
  local copies, waits for them, and re-layouts  19.7 us (3%)
  between operations  15.4 us (2%)
    unnamed x4, waiting for transfers between devices  349 us
    unnamed x1, blocking collectives  61.9 us
    all_gather x1, blocking collectives, shards(): lax.all_gather(linear_basis, 'snaps', axis=0, tiled=True)  39.7 us
    all_gather x1, blocking collectives, shards(): lax.all_gather(quad_weights, 'snaps', axis=0, tiled=True)  35 us
    dot_general x8, matrix products, block_core(): lax.dot_general(tail_f32, back_quad * lead_vals, contract_rows, precision...  21.8 us
    dot_general x8, matrix products, block_step(): lax.dot_general(residual, quad_block, contract_cols, preferred_element_ty...  20.5 us
    dot_general x8, matrix products, block_core(): jnp.dot(lead_bf16, coord_block, preferred_element_type=jnp.float32)  20.2 us
    dot_general x8, matrix products, block_core(): lax.dot_general(lead_f32, back_quad * tail_vals, contract_rows, precision...  16.6 us
  transfers between devices with their start and end apart: 2, of which 2 were waited for; matrix products, arithmetic and copies ran while one was open for 1% of the time, Pallas kernels for 0%

commit v1 on v0

--- a/solution.py
+++ b/solution.py
@@ -26,10 +26,12 @@
     tail_f32 = jnp.asarray(tail_np)
     lead_bf16 = lead_f32.astype(jnp.bfloat16)
     tail_bf16 = tail_f32.astype(jnp.bfloat16)
-    lin_rows, quad_rows = (
-        lax.all_gather(linear_basis, "snaps", axis=0, tiled=True),
-        lax.all_gather(quad_weights, "snaps", axis=0, tiled=True),
-    )
+    snap_parts = lax.axis_size("snaps")
+    row_parts = lax.axis_size("rows")
+    own_maps = jnp.concatenate([linear_basis, quad_weights], axis=1)
+    own_maps = jnp.broadcast_to(own_maps[None], (snap_parts,) + own_maps.shape)
+    maps = lax.all_to_all(own_maps, "snaps", 0, 0, tiled=True).reshape(local_rows, -1)
+    lin_rows, quad_rows = maps[:, :coord_count], maps[:, coord_count:]
     block_width = min(256, snap_dev)
     block_total = snap_dev // block_width
     contract_rows = (((0,), (0,)), ((), ()))
@@ -77,12 +79,13 @@
         jnp.zeros((coord_count, snap_dev), jnp.float32),
     )
     lin_grad, quad_grad, coord_part = lax.fori_loop(0, block_total, block_step, start_state)
-    lin_sum, quad_sum = (
-        lax.psum_scatter(lin_grad, "snaps", scatter_dimension=0, tiled=True),
-        lax.psum_scatter(quad_grad, "snaps", scatter_dimension=0, tiled=True),
-    )
-    coord_share = lax.psum_scatter(coord_part, "rows", scatter_dimension=0, tiled=True)
-    grad_coords = coord_share * (1.0 / math.sqrt(local_rows * lax.axis_size("rows")))
+    model_grad = jnp.concatenate([lin_grad, quad_grad], axis=1)
+    model_grad = model_grad.reshape(snap_parts, -1, model_grad.shape[1])
+    model_sum = jnp.sum(lax.all_to_all(model_grad, "snaps", 0, 0, tiled=True), axis=0)
+    lin_sum, quad_sum = model_sum[:, :coord_count], model_sum[:, coord_count:]
+    coord_part = coord_part.reshape(row_parts, -1, snap_dev)
+    coord_share = jnp.sum(lax.all_to_all(coord_part, "rows", 0, 0, tiled=True), axis=0)
+    grad_coords = coord_share * (1.0 / math.sqrt(local_rows * row_parts))
     model_scale = 1.0 / math.sqrt(snap_dev * lax.axis_size("snaps"))
     return (lin_sum * model_scale, quad_sum * model_scale, grad_coords)
 

time: 651 us -> 206 us (0.32)
  the two profiles are of different devices: /device:TPU:4 before, /device:TPU:8 now
where the time goes in v1:
time: 206 us; the launch traced here: 203 us
  matrix products  88 us (43%)
  waiting for transfers between devices  64.1 us (31%)
  starting transfers between devices  24.9 us (12%)
  local copies, waits for them, and re-layouts  19.9 us (10%)
  other arithmetic  4.37 us (2%)
    all_to_all x1, waiting for transfers between devices, shards(): lax.all_to_all(model_grad, 'snaps', 0, 0, tiled=True)  28.6 us
    dot_general x8, matrix products, block_core(): lax.dot_general(tail_f32, back_quad * lead_vals, contract_rows, precision...  21.9 us
    all_to_all x1, waiting for transfers between devices, shards(): lax.all_to_all(own_maps, 'snaps', 0, 0, tiled=True).reshape(local_rows, -1)  18.1 us
    all_to_all x1, waiting for transfers between devices, shards(): lax.all_to_all(coord_part, 'rows', 0, 0, tiled=True)  17.4 us
    dot_general x8, matrix products, block_core(): lax.dot_general(lead_f32, back_quad * tail_vals, contract_rows, precision...  16.7 us
    dot_general x8, matrix products, block_core(): jnp.dot(tail_bf16, coord_block, preferred_element_type=jnp.float32)  11.7 us
    all_to_all x1, starting transfers between devices, shards(): lax.all_to_all(own_maps, 'snaps', 0, 0, tiled=True).reshape(local_rows, -1)  11.3 us
    all_to_all x1, starting transfers between devices, shards(): lax.all_to_all(coord_part, 'rows', 0, 0, tiled=True)  9.87 us
  transfers between devices with their start and end apart: 3, of which 3 were waited for; matrix products, arithmetic and copies ran while one was open for 1% of the time, Pallas kernels for 0%

profile of v1, /device:TPU:8, one launch (start us, length us, event | category | flops | bytes accessed | tf_op | source)
XLA Modules:
  0.0 202.6 jit_solution(3852277091763845207)
XLA Ops:
  2.3 11.3 %all-to-all-start = ((bf16[16,8,2144]{2,1,0:T(8,128)(2,1)}), bf16[16,8,2144]{2,1,0:T(8,128)(2,1)S(1)}, u32[]{:S(2)}, u32[]{:S(2)}) async-start(bf16[16,8,2144]{2,1,0:T(8,128)(2,1)} %broadcast_in_dim.18), calls=%async_computation | async-start | bytes 1114112 | tf_op jit(solution)/shard_map/all_to_all | solution.py:33
  13.7 18.1 %all-to-all-done = bf16[16,8,2144]{2,1,0:T(8,128)(2,1)S(1)} async-done(((bf16[16,8,2144]{2,1,0:T(8,128)(2,1)}), bf16[16,8,2144]{2,1,0:T(8,128)(2,1)S(1)}, u32[]{:S(2)}, u32[]{:S(2)}) %all-to-all-start) | async-done | bytes 548896 | tf_op jit(solution)/shard_map/all_to_all | solution.py:33
  34.8 102.1 %while.20 = (s32[]{:T(128)}, f32[128,64]{0,1:T(8,128)S(1)}, f32[128,2080]{0,1:T(8,128)S(1)}, f32[64,2048]{1,0:T(8,128)}, bf16[64,2048]{1,0:T(8,128)(2,1)}, /*ind...) while((s32[]{:T(128)}, f32[128,64]{0,1:T(8,128)S(1)}, ...), condition=%wide.region_1.0_spmd.clone.clone.clone, body=%wide.region_0.0_spmd.sunk.clone.clone.clone.sunk | while | flops 1378574336 | bytes 28897544 | solution.py:81
  42.7 2.1 %fusion.100 = f32[256,64]{0,1:T(8,128)S(1)} fusion(f32[256,64]{0,1:T(8,128)S(1)} %fusion.98, f32[2080,64]{1,0:T(8,128)S(1)} %copy-done.1, f32[256,2080]{0,1:T(8,128)S(1)} %fusion.99, f32[256,2080]{0,1:T(8,128)S(1)} %fusion.96), kind=kOutput, calls=%fused_computation.12.clone.1 | convolution fusion | flops 409493504 | bytes 4923392 | tf_op jit(solution)/shard_map/while/body/eval_jaxpr/dot_general | solution.py:55
  44.8 2.7 %fusion.101 = f32[64,2048]{1,0:T(8,128)} fusion(f32[64,2048]{1,0:T(8,128)} %get-tuple-element.432, s32[]{:T(128)S(6)} %select_n.14, f32[256,64]{0,1:T(8,128)S(1)} %fusion.100, f32[2080,64]{1,0:T(8,128)S(1)} %get-tuple-element.460, f32[256,2080]{0,1:T(8,128)S(1)} %fusion.99, f32[256,2080]{0,1:T(8,128)S(1)} %get-tuple-element.412), kind=kOutput, calls=%fused_computation.15.clone.1 | convolution fusion | flops 409493504 | bytes 4923396 | tf_op jit(solution)/shard_map/while/body/eval_jaxpr/dot_general | solution.py:58
  55.4 2.1 %fusion.100 = f32[256,64]{0,1:T(8,128)S(1)} fusion(f32[256,64]{0,1:T(8,128)S(1)} %fusion.98, f32[2080,64]{1,0:T(8,128)S(1)} %copy-done.1, f32[256,2080]{0,1:T(8,128)S(1)} %fusion.99, f32[256,2080]{0,1:T(8,128)S(1)} %fusion.96), kind=kOutput, calls=%fused_computation.12.clone.1 | convolution fusion | flops 409493504 | bytes 4923392 | tf_op jit(solution)/shard_map/while/body/eval_jaxpr/dot_general | solution.py:55
  57.5 2.7 %fusion.101 = f32[64,2048]{1,0:T(8,128)} fusion(f32[64,2048]{1,0:T(8,128)} %get-tuple-element.432, s32[]{:T(128)S(6)} %select_n.14, f32[256,64]{0,1:T(8,128)S(1)} %fusion.100, f32[2080,64]{1,0:T(8,128)S(1)} %get-tuple-element.460, f32[256,2080]{0,1:T(8,128)S(1)} %fusion.99, f32[256,2080]{0,1:T(8,128)S(1)} %get-tuple-element.412), kind=kOutput, calls=%fused_computation.15.clone.1 | convolution fusion | flops 409493504 | bytes 4923396 | tf_op jit(solution)/shard_map/while/body/eval_jaxpr/dot_general | solution.py:58
  68.2 2.1 %fusion.100 = f32[256,64]{0,1:T(8,128)S(1)} fusion(f32[256,64]{0,1:T(8,128)S(1)} %fusion.98, f32[2080,64]{1,0:T(8,128)S(1)} %copy-done.1, f32[256,2080]{0,1:T(8,128)S(1)} %fusion.99, f32[256,2080]{0,1:T(8,128)S(1)} %fusion.96), kind=kOutput, calls=%fused_computation.12.clone.1 | convolution fusion | flops 409493504 | bytes 4923392 | tf_op jit(solution)/shard_map/while/body/eval_jaxpr/dot_general | solution.py:55
  70.3 2.7 %fusion.101 = f32[64,2048]{1,0:T(8,128)} fusion(f32[64,2048]{1,0:T(8,128)} %get-tuple-element.432, s32[]{:T(128)S(6)} %select_n.14, f32[256,64]{0,1:T(8,128)S(1)} %fusion.100, f32[2080,64]{1,0:T(8,128)S(1)} %get-tuple-element.460, f32[256,2080]{0,1:T(8,128)S(1)} %fusion.99, f32[256,2080]{0,1:T(8,128)S(1)} %get-tuple-element.412), kind=kOutput, calls=%fused_computation.15.clone.1 | convolution fusion | flops 409493504 | bytes 4923396 | tf_op jit(solution)/shard_map/while/body/eval_jaxpr/dot_general | solution.py:58
  81.0 2.1 %fusion.100 = f32[256,64]{0,1:T(8,128)S(1)} fusion(f32[256,64]{0,1:T(8,128)S(1)} %fusion.98, f32[2080,64]{1,0:T(8,128)S(1)} %copy-done.1, f32[256,2080]{0,1:T(8,128)S(1)} %fusion.99, f32[256,2080]{0,1:T(8,128)S(1)} %fusion.96), kind=kOutput, calls=%fused_computation.12.clone.1 | convolution fusion | flops 409493504 | bytes 4923392 | tf_op jit(solution)/shard_map/while/body/eval_jaxpr/dot_general | solution.py:55
  83.1 2.7 %fusion.101 = f32[64,2048]{1,0:T(8,128)} fusion(f32[64,2048]{1,0:T(8,128)} %get-tuple-element.432, s32[]{:T(128)S(6)} %select_n.14, f32[256,64]{0,1:T(8,128)S(1)} %fusion.100, f32[2080,64]{1,0:T(8,128)S(1)} %get-tuple-element.460, f32[256,2080]{0,1:T(8,128)S(1)} %fusion.99, f32[256,2080]{0,1:T(8,128)S(1)} %get-tuple-element.412), kind=kOutput, calls=%fused_computation.15.clone.1 | convolution fusion | flops 409493504 | bytes 4923396 | tf_op jit(solution)/shard_map/while/body/eval_jaxpr/dot_general | solution.py:58
  93.8 2.1 %fusion.100 = f32[256,64]{0,1:T(8,128)S(1)} fusion(f32[256,64]{0,1:T(8,128)S(1)} %fusion.98, f32[2080,64]{1,0:T(8,128)S(1)} %copy-done.1, f32[256,2080]{0,1:T(8,128)S(1)} %fusion.99, f32[256,2080]{0,1:T(8,128)S(1)} %fusion.96), kind=kOutput, calls=%fused_computation.12.clone.1 | convolution fusion | flops 409493504 | bytes 4923392 | tf_op jit(solution)/shard_map/while/body/eval_jaxpr/dot_general | solution.py:55
  95.9 2.7 %fusion.101 = f32[64,2048]{1,0:T(8,128)} fusion(f32[64,2048]{1,0:T(8,128)} %get-tuple-element.432, s32[]{:T(128)S(6)} %select_n.14, f32[256,64]{0,1:T(8,128)S(1)} %fusion.100, f32[2080,64]{1,0:T(8,128)S(1)} %get-tuple-element.460, f32[256,2080]{0,1:T(8,128)S(1)} %fusion.99, f32[256,2080]{0,1:T(8,128)S(1)} %get-tuple-element.412), kind=kOutput, calls=%fused_computation.15.clone.1 | convolution fusion | flops 409493504 | bytes 4923396 | tf_op jit(solution)/shard_map/while/body/eval_jaxpr/dot_general | solution.py:58
  106.5 2.1 %fusion.100 = f32[256,64]{0,1:T(8,128)S(1)} fusion(f32[256,64]{0,1:T(8,128)S(1)} %fusion.98, f32[2080,64]{1,0:T(8,128)S(1)} %copy-done.1, f32[256,2080]{0,1:T(8,128)S(1)} %fusion.99, f32[256,2080]{0,1:T(8,128)S(1)} %fusion.96), kind=kOutput, calls=%fused_computation.12.clone.1 | convolution fusion | flops 409493504 | bytes 4923392 | tf_op jit(solution)/shard_map/while/body/eval_jaxpr/dot_general | solution.py:55
  108.6 2.7 %fusion.101 = f32[64,2048]{1,0:T(8,128)} fusion(f32[64,2048]{1,0:T(8,128)} %get-tuple-element.432, s32[]{:T(128)S(6)} %select_n.14, f32[256,64]{0,1:T(8,128)S(1)} %fusion.100, f32[2080,64]{1,0:T(8,128)S(1)} %get-tuple-element.460, f32[256,2080]{0,1:T(8,128)S(1)} %fusion.99, f32[256,2080]{0,1:T(8,128)S(1)} %get-tuple-element.412), kind=kOutput, calls=%fused_computation.15.clone.1 | convolution fusion | flops 409493504 | bytes 4923396 | tf_op jit(solution)/shard_map/while/body/eval_jaxpr/dot_general | solution.py:58
  119.3 2.1 %fusion.100 = f32[256,64]{0,1:T(8,128)S(1)} fusion(f32[256,64]{0,1:T(8,128)S(1)} %fusion.98, f32[2080,64]{1,0:T(8,128)S(1)} %copy-done.1, f32[256,2080]{0,1:T(8,128)S(1)} %fusion.99, f32[256,2080]{0,1:T(8,128)S(1)} %fusion.96), kind=kOutput, calls=%fused_computation.12.clone.1 | convolution fusion | flops 409493504 | bytes 4923392 | tf_op jit(solution)/shard_map/while/body/eval_jaxpr/dot_general | solution.py:55
  121.4 2.7 %fusion.101 = f32[64,2048]{1,0:T(8,128)} fusion(f32[64,2048]{1,0:T(8,128)} %get-tuple-element.432, s32[]{:T(128)S(6)} %select_n.14, f32[256,64]{0,1:T(8,128)S(1)} %fusion.100, f32[2080,64]{1,0:T(8,128)S(1)} %get-tuple-element.460, f32[256,2080]{0,1:T(8,128)S(1)} %fusion.99, f32[256,2080]{0,1:T(8,128)S(1)} %get-tuple-element.412), kind=kOutput, calls=%fused_computation.15.clone.1 | convolution fusion | flops 409493504 | bytes 4923396 | tf_op jit(solution)/shard_map/while/body/eval_jaxpr/dot_general | solution.py:58
  132.0 2.1 %fusion.100 = f32[256,64]{0,1:T(8,128)S(1)} fusion(f32[256,64]{0,1:T(8,128)S(1)} %fusion.98, f32[2080,64]{1,0:T(8,128)S(1)} %copy-done.1, f32[256,2080]{0,1:T(8,128)S(1)} %fusion.99, f32[256,2080]{0,1:T(8,128)S(1)} %fusion.96), kind=kOutput, calls=%fused_computation.12.clone.1 | convolution fusion | flops 409493504 | bytes 4923392 | tf_op jit(solution)/shard_map/while/body/eval_jaxpr/dot_general | solution.py:55
  134.1 2.8 %fusion.101 = f32[64,2048]{1,0:T(8,128)} fusion(f32[64,2048]{1,0:T(8,128)} %get-tuple-element.432, s32[]{:T(128)S(6)} %select_n.14, f32[256,64]{0,1:T(8,128)S(1)} %fusion.100, f32[2080,64]{1,0:T(8,128)S(1)} %get-tuple-element.460, f32[256,2080]{0,1:T(8,128)S(1)} %fusion.99, f32[256,2080]{0,1:T(8,128)S(1)} %get-tuple-element.412), kind=kOutput, calls=%fused_computation.15.clone.1 | convolution fusion | flops 409493504 | bytes 4923396 | tf_op jit(solution)/shard_map/while/body/eval_jaxpr/dot_general | solution.py:58
  136.9 2.2 %reshape.18 = f32[32,2,2048]{2,1,0:T(2,128)} reshape(f32[64,2048]{1,0:T(8,128)} %get-tuple-element.206) | data formatting | bytes 1048576 | tf_op jit(solution)/shard_map/reshape | solution.py:86
  139.1 9.9 %all-to-all-start.2 = ((f32[32,2,2048]{2,1,0:T(2,128)}), f32[32,2,2048]{2,1,0:T(2,128)S(1)}, u32[]{:S(2)}, u32[]{:S(2)}) async-start(f32[32,2,2048]{2,1,0:T(2,128)} %reshape.18), calls=%async_computation.2 | async-start | bytes 1048576 | tf_op jit(solution)/shard_map/all_to_all | solution.py:87
  150.8 17.4 %all-to-all-done.2 = f32[32,2,2048]{2,1,0:T(2,128)S(1)} async-done(((f32[32,2,2048]{2,1,0:T(2,128)}), f32[32,2,2048]{2,1,0:T(2,128)S(1)}, u32[]{:S(2)}, u32[]{:S(2)}) %all-to-all-start.2) | async-done | bytes 524320 | tf_op jit(solution)/shard_map/all_to_all | solution.py:87
  168.2 3.7 %all-to-all-start.1 = ((f32[16,8,2144]{2,1,0:T(8,128)}), f32[16,8,2144]{2,1,0:T(8,128)S(1)}, u32[]{:S(2)}, u32[]{:S(2)}) async-start(f32[16,8,2144]{2,1,0:T(8,128)} %maximum_bitcast_fusion), calls=%async_computation.1 | async-start | bytes 2228224 | tf_op jit(solution)/shard_map/all_to_all | solution.py:84
  172.7 28.6 %all-to-all-done.1 = f32[16,8,2144]{2,1,0:T(8,128)S(1)} async-done(((f32[16,8,2144]{2,1,0:T(8,128)}), f32[16,8,2144]{2,1,0:T(8,128)S(1)}, u32[]{:S(2)}, u32[]{:S(2)}) %all-to-all-start.1) | async-done | bytes 1097760 | tf_op jit(solution)/shard_map/all_to_all | solution.py:84
  (117 shorter events, 71.6 us)
Async XLA Ops:
  2.3 29.5 %all-to-all-start = ((bf16[16,8,2144]{2,1,0:T(8,128)(2,1)}), bf16[16,8,2144]{2,1,0:T(8,128)(2,1)S(1)}, u32[]{:S(2)}, u32[]{:S(2)}) async-start(bf16[16,8,2144]{2,1,0:T(8,128)(2,1)} %broadcast_in_dim.18), calls=%async_computation | async-start | bytes 1114112 | tf_op jit(solution)/shard_map/all_to_all | solution.py:33
  13.7 21.1 %copy-start = (f32[2080,64]{1,0:T(8,128)S(1)}, f32[2080,64]{1,0:T(8,128)}, u32[]{:S(2)}) copy-start(f32[2080,64]{1,0:T(8,128)} %constant.45.clone..sunk.4) | copy-start | bytes 1597444
  13.7 21.0 %copy-start.2 = (bf16[2080,64]{1,0:T(8,128)(2,1)S(1)}, bf16[2080,64]{1,0:T(8,128)(2,1)}, u32[]{:S(2)}) copy-start(bf16[2080,64]{1,0:T(8,128)(2,1)} %constant.80) | copy-start | bytes 798724
  31.8 0.8 copy-start.3
  41.5 1.2 copy-start.1
  54.2 1.2 copy-start.1
  67.0 1.2 copy-start.1
  79.8 1.2 copy-start.1
  92.5 1.2 copy-start.1
  105.3 1.2 copy-start.1
  118.0 1.2 copy-start.1
  130.8 1.2 copy-start.1
  139.1 29.1 %all-to-all-start.2 = ((f32[32,2,2048]{2,1,0:T(2,128)}), f32[32,2,2048]{2,1,0:T(2,128)S(1)}, u32[]{:S(2)}, u32[]{:S(2)}) async-start(f32[32,2,2048]{2,1,0:T(2,128)} %reshape.18), calls=%async_computation.2 | async-start | bytes 1048576 | tf_op jit(solution)/shard_map/all_to_all | solution.py:87
  168.2 33.1 %all-to-all-start.1 = ((f32[16,8,2144]{2,1,0:T(8,128)}), f32[16,8,2144]{2,1,0:T(8,128)S(1)}, u32[]{:S(2)}, u32[]{:S(2)}) async-start(f32[16,8,2144]{2,1,0:T(8,128)} %maximum_bitcast_fusion), calls=%async_computation.1 | async-start | bytes 2228224 | tf_op jit(solution)/shard_map/all_to_all | solution.py:84

commit v2 on v1

v2 whole, which is shorter than its diff:
```python
import math

import jax
import jax.numpy as jnp
import numpy as np
from jax import lax
from jax.experimental import pallas as pl
from jax.experimental.pallas import tpu as pltpu
from jax.sharding import PartitionSpec as P


LANES = 128
BLOCK = 256
WIDE = 512
TOP = 14.0
CORES, FAR, RING = 2, 2, 8


def coordinate_order(count):
    each = count // (CORES * FAR * RING)
    return np.arange(count).reshape(FAR, RING, CORES, each).transpose(2, 0, 1, 3).reshape(-1)


def column_source(count):
    order = coordinate_order(count)
    offset = np.cumsum([0] + [count - i for i in range(count)])
    source = []
    for d in range(count // 2 + 1):
        for k in range(count):
            i, j = sorted((order[k], order[(k + d) % count]))
            source.append(-1 if d == count // 2 and k >= d else offset[i] + j - i)
    return np.concatenate([source, offset[-1] + order])


def gather_tables(source):
    pad = -len(source) % LANES
    source = np.concatenate([source, np.full(pad, -1)]).reshape(-1, 1, LANES)
    source = np.broadcast_to(source, (source.shape[0], 8, LANES)).astype(np.int32)
    return np.where(source < 0, 0, source % LANES), np.where(source < 0, -1, source // LANES)


def permuted(tiles, lane, tile):
    total = jnp.zeros(tiles[0].shape, jnp.float32)
    for number, values in enumerate(tiles):
        moved = jnp.take_along_axis(values, lane, axis=1)
        total = jnp.where(tile == number, moved, total)
    return total


def tiles_of(values):
    return [values[:, t : t + LANES] for t in range(0, values.shape[1], LANES)]


def spread_kernel(lin_ref, quad_ref, lane_ref, tile_ref, out_ref, wide_ref):
    pairs = quad_ref.shape[1]
    wide_ref[...] = jnp.zeros_like(wide_ref)
    wide_ref[:, :pairs] = quad_ref[...].astype(jnp.float32)
    wide_ref[:, pairs : pairs + lin_ref.shape[1]] = lin_ref[...].astype(jnp.float32)
    tiles = tiles_of(wide_ref[...])
    for t in range(lane_ref.shape[0]):
        moved = permuted(tiles, lane_ref[t], tile_ref[t]).astype(jnp.bfloat16)
        for c in range(out_ref.shape[0]):
            out_ref[c, :, t * LANES : (t + 1) * LANES] = moved


def turned(values, count, step):
    step %= count
    return values if step == 0 else jnp.concatenate([values[step:], values[:step]], axis=0)


def forward_kernel(pairs, maps_ref, coord_ref, snap_ref, grad_ref, res_ref, feat_ref):
    count, columns = coord_ref.shape
    rows, width = maps_ref.shape
    blocks = [slice(n, n + WIDE) for n in range(0, columns, WIDE)]

    def features(block):
        for start in range(block.start, block.stop, LANES):
            part = slice(start, start + LANES)
            coord = coord_ref[:, part].astype(jnp.float32)
            for r in range(8):
                shifted = coord if r == 0 else pltpu.roll(coord, count - r, 0)
                for d in range(r, count // 2 + 1, 8):
                    feat_ref[d * count : (d + 1) * count, part] = (
                        coord * turned(shifted, count, d - r)
                    ).astype(jnp.bfloat16)
            feat_ref[width - count :, part] = coord_ref[:, part]

    features(blocks[0])
    for n, block in enumerate(blocks):
        rebuilt = jnp.dot(maps_ref[...], feat_ref[:, block], preferred_element_type=jnp.float32)
        if n + 1 < len(blocks):
            features(blocks[n + 1])
        res_ref[:, block] = (rebuilt - snap_ref[:, block].astype(jnp.float32)).astype(jnp.bfloat16)
    top = jnp.zeros((rows, LANES), jnp.float32)
    for start in range(0, width, WIDE):
        part = slice(start, min(start + WIDE, width))
        grad = lax.dot_general(
            res_ref[...], feat_ref[part], (((1,), (1,)), ((), ())), preferred_element_type=jnp.float32
        )
        grad_ref[:, part] = grad
        for tile in tiles_of(grad):
            top = jnp.maximum(top, jnp.abs(tile))
    top = jnp.max(jnp.max(top, axis=0, keepdims=True), axis=1, keepdims=True)
    level = jnp.floor(jnp.log2(jnp.maximum(top, 2.0**-100)))
    scale = jnp.exp2(TOP - level)
    for start in range(0, width, LANES):
        part = slice(start, start + LANES)
        values = grad_ref[:, part] * scale
        if start <= pairs < start + LANES:
            lane = lax.broadcasted_iota(jnp.int32, values.shape, 1) + start
            values = jnp.where((lane >= pairs) & (lane < width - count), level, values)
        grad_ref[:, part] = values


def backward_kernel(scale, maps_ref, coord_ref, res_ref, out_ref, turn_ref):
    count = coord_ref.shape[0]
    width = maps_ref.shape[1]

    @pl.when(pl.program_id(0) == 0)
    def _():
        turn_ref[...] = maps_ref[...].astype(jnp.float32).T.astype(jnp.bfloat16)

    coord = coord_ref[...].astype(jnp.float32)
    residual = res_ref[...]

    def back(row):
        return jnp.dot(turn_ref[row : row + count], residual, preferred_element_type=jnp.float32)

    total = back(width - count)
    for r in range(8):
        shifted = coord if r == 0 else pltpu.roll(coord, count - r, 0)
        spun = jnp.zeros_like(coord)
        for d in range(r, count // 2 + 1, 8):
            part = back(d * count)
            total = total + part * turned(shifted, count, d - r)
            spun = spun + turned(part * coord, count, r - d)
        total = total + (spun if r == 0 else pltpu.roll(spun, r, 0))
    out_ref[...] = total * scale


def gather_kernel(scale, parts_ref, lane_ref, tile_ref, lin_ref, quad_ref, wide_ref):
    pairs = quad_ref.shape[1]
    total = jnp.zeros(parts_ref.shape[1:], jnp.float32)
    for p in range(parts_ref.shape[0]):
        part = parts_ref[p]
        total = total + part * jnp.exp2(part[:, pairs : pairs + 1] - TOP)
    tiles = tiles_of(total * scale)
    for t in range(lane_ref.shape[0]):
        wide_ref[:, t * LANES : (t + 1) * LANES] = permuted(tiles, lane_ref[t], tile_ref[t])
    quad_ref[...] = wide_ref[:, :pairs]
    lin_ref[...] = wide_ref[:, pairs : pairs + lin_ref.shape[1]]


def shards(snapshots, linear_basis, quad_weights, coordinates):
    count = coordinates.shape[0]
    local_rows, snap_dev = snapshots.shape
    own_rows, pairs = quad_weights.shape
    snap_parts = lax.axis_size("snaps")
    row_parts = lax.axis_size("rows")
    assert row_parts == CORES * FAR * RING and (pairs + count) % 32 == 0
    source = column_source(count)
    width = len(source)
    padded = pairs + count + -(pairs + count) % LANES
    lane, tile = gather_tables(source)
    back_source = np.zeros(pairs + count, np.int64)
    back_source[source[source >= 0]] = np.nonzero(source >= 0)[0]
    back_lane, back_tile = gather_tables(back_source)

    own = pl.pallas_call(
        spread_kernel,
        out_shape=jax.ShapeDtypeStruct((snap_parts, own_rows, width), jnp.bfloat16),
        scratch_shapes=[pltpu.VMEM((own_rows, padded), jnp.float32)],
    )(linear_basis, quad_weights, jnp.asarray(lane), jnp.asarray(tile))
    maps = lax.all_to_all(own, "snaps", 0, 0, tiled=True).reshape(local_rows, width)
    coords = coordinates.reshape(FAR, RING, CORES, -1, snap_dev).transpose(2, 0, 1, 3, 4).reshape(count, snap_dev)

    flops = 2 * local_rows * width * snap_dev
    grad, residual = pl.pallas_call(
        lambda *refs: forward_kernel(pairs, *refs),
        out_shape=[
            jax.ShapeDtypeStruct((local_rows, width), jnp.float32),
            jax.ShapeDtypeStruct((local_rows, snap_dev), jnp.bfloat16),
        ],
        scratch_shapes=[pltpu.VMEM((width, snap_dev), jnp.bfloat16)],
        compiler_params=pltpu.CompilerParams(vmem_limit_bytes=24 << 20),
        cost_estimate=pl.CostEstimate(flops=2 * flops, bytes_accessed=4 << 20, transcendentals=0),
    )(maps, coords, snapshots)
    grad = grad.astype(jnp.float16).reshape(snap_parts, own_rows, width)
    grad_parts = lax.all_to_all(grad, "snaps", 0, 0, tiled=True)

    block = min(BLOCK, snap_dev)
    coord_scale = 1.0 / math.sqrt(local_rows * row_parts)
    coord_part = pl.pallas_call(
        lambda *refs: backward_kernel(coord_scale, *refs),
        grid=(snap_dev // block,),
        in_specs=[
            pl.BlockSpec((local_rows, width), lambda n: (0, 0), pipeline_mode=pl.Buffered(1)),
            pl.BlockSpec((count, block), lambda n: (0, n)),
            pl.BlockSpec((local_rows, block), lambda n: (0, n)),
        ],
        out_specs=pl.BlockSpec((count, block), lambda n: (0, n)),
        out_shape=jax.ShapeDtypeStruct((count, snap_dev), jnp.float32),
        scratch_shapes=[pltpu.VMEM((width, local_rows), jnp.bfloat16)],
        compiler_params=pltpu.CompilerParams(vmem_limit_bytes=24 << 20),
        cost_estimate=pl.CostEstimate(flops=flops, bytes_accessed=2 << 20, transcendentals=0),
    )(maps, coords, residual)

    place = lax.axis_index("rows")
    for apart, own_half in ((1, place % CORES), (CORES * RING, place // (CORES * RING))):
        half = coord_part.shape[0] // 2
        sent = lax.dynamic_slice_in_dim(coord_part, (1 - own_half) * half, half, 0)
        kept = lax.dynamic_slice_in_dim(coord_part, own_half * half, half, 0)
        came = lax.ppermute(sent, "rows", [(i, i ^ apart) for i in range(row_parts)])
        coord_part = kept + came
    rings = [[(f * RING + y) * CORES + c for y in range(RING)] for f in range(FAR) for c in range(CORES)]
    coord_parts = lax.all_to_all(
        coord_part.reshape(RING, -1, snap_dev), "rows", 0, 0, axis_index_groups=rings, tiled=True
    )
    grad_coords = jnp.sum(coord_parts, axis=0)

    model_scale = 1.0 / math.sqrt(snap_dev * snap_parts)
    grad_basis, grad_quad = pl.pallas_call(
        lambda *refs: gather_kernel(model_scale, *refs),
        out_shape=[
            jax.ShapeDtypeStruct(linear_basis.shape, jnp.float32),
            jax.ShapeDtypeStruct(quad_weights.shape, jnp.float32),
        ],
        scratch_shapes=[pltpu.VMEM((own_rows, padded), jnp.float32)],
    )(grad_parts.astype(jnp.float32), jnp.asarray(back_lane), jnp.asarray(back_tile))
    return (grad_basis, grad_quad, grad_coords)


def solution(mesh):
    placed = (
        P("rows", "snaps"),
        P(("rows", "snaps"), None),
        P(("rows", "snaps"), None),
        P(None, "snaps"),
    )

    return jax.shard_map(
        shards,
        mesh=mesh,
        in_specs=placed,
        out_specs=(P(("rows", "snaps"), None), P(("rows", "snaps"), None), P("rows", "snaps")),
        check_vma=False,
    )
```

time: 206 us -> 97.3 us (0.47)
  the two profiles are of different devices: /device:TPU:8 before, /device:TPU:4 now
where the time goes in v2:
time: 97.3 us; the launch traced here: 96.8 us
  waiting for transfers between devices  49.7 us (51%)
  starting transfers between devices  26.5 us (27%)
  Pallas kernels  15.9 us (16%)
  other arithmetic  2.62 us (3%)
  local copies, waits for them, and re-layouts  1.24 us (1%)
    all_to_all x1, waiting for transfers between devices, shards(): lax.all_to_all(own, 'snaps', 0, 0, tiled=True).reshape(local_rows, width)  17.6 us
    all_to_all x1, waiting for transfers between devices, shards(): grad_parts = lax.all_to_all(grad, 'snaps', 0, 0, tiled=True)  16.2 us
    all_to_all x1, starting transfers between devices, shards(): lax.all_to_all(own, 'snaps', 0, 0, tiled=True).reshape(local_rows, width)  11.2 us
    all_to_all x1, waiting for transfers between devices, shards(): lax.all_to_all(coord_part.reshape(RING, -1, snap_dev), 'rows', 0, 0, axis...  8.22 us
    ppermute x2, waiting for transfers between devices, shards(): lax.ppermute(sent, 'rows', [(i, i ^ apart) for i in range(row_parts)])  7.67 us
    all_to_all x1, starting transfers between devices, shards(): lax.all_to_all(coord_part.reshape(RING, -1, snap_dev), 'rows', 0, 0, axis...  7.11 us
    pallas_call x1, Pallas kernels, shards(): pl.pallas_call(lambda *refs: forward_kernel(pairs, *refs), out_shape=[jax...  6.25 us
    pallas_call x1, Pallas kernels, shards(): pl.pallas_call(lambda *refs: backward_kernel(coord_scale, *refs), grid=(s...  5.06 us
  transfers between devices with their start and end apart: 5, of which 5 were waited for; matrix products, arithmetic and copies ran while one was open for 2% of the time, Pallas kernels for 0%

profile of v2, /device:TPU:4, one launch (start us, length us, event | category | flops | bytes accessed | tf_op | source)
XLA Modules:
  0.0 96.8 jit_solution(4762395499375543700)
XLA Ops:
  0.6 0.0 copy-start.1
  0.6 2.1 %shard_map.103 = bf16[16,8,2176]{2,1,0:T(8,128)(2,1)} custom-call(bf16[8,64]{1,0:T(8,128)(2,1)} %lin_ref.1, bf16[8,2080]{1,0:T(8,128)(2,1)} %quad_ref.1, s32[17,8,128]{2,1,0:T(8,128)} %constant.50.clone.lane_ref, s32[17,8,128]{2,1,0:T(8,128)} %constant.51.clone.tile_ref), custom_call_target="tpu_custom_call" | custom-call | tf_op jit(solution)/shard_map/pallas_call | solution.py:169
  2.7 11.2 %all-to-all-start = ((bf16[16,8,2176]{2,1,0:T(8,128)(2,1)}), bf16[16,8,2176]{2,1,0:T(8,128)(2,1)S(1)}, u32[]{:S(2)}, u32[]{:S(2)}) async-start(bf16[16,8,2176]{2,1,0:T(8,128)(2,1)} %shard_map.103), calls=%async_computation | async-start | bytes 1114112 | tf_op jit(solution)/shard_map/all_to_all | solution.py:174
  13.9 0.0 copy-done.1
  14.0 0.2 reshape.22
  14.1 0.2 copy.13
  14.3 0.1 reshape.23.refs_1_
  14.5 17.6 %all-to-all-done = bf16[16,8,2176]{2,1,0:T(8,128)(2,1)S(1)} async-done(((bf16[16,8,2176]{2,1,0:T(8,128)(2,1)}), bf16[16,8,2176]{2,1,0:T(8,128)(2,1)S(1)}, u32[]{:S(2)}, u32[]{:S(2)}) %all-to-all-start) | async-done | bytes 557088 | tf_op jit(solution)/shard_map/all_to_all | solution.py:174
  32.1 0.0 copy-done
  32.1 6.3 %shard_map.104 = (f32[128,2176]{1,0:T(8,128)S(1)}, bf16[128,2048]{1,0:T(8,128)(2,1)S(1)}) custom-call(bf16[128,2176]{1,0:T(8,128)(2,1)S(1)} %bitcast.6, bf16[64,2048]{1,0:T(8,128)(2,1)S(1)} %reshape.23.refs_1_, bf16[128,2048]{1,0:T(8,128)(2,1)S(1)} %copy-done), custom_call_target="tpu_custom_call" | custom-call | flops 2281701376 | bytes 4194304 | tf_op jit(solution)/shard_map/pallas_call | solution.py:178
  38.3 5.1 %shard_map.106 = f32[64,2048]{1,0:T(8,128)S(1)} custom-call(bf16[128,2176]{1,0:T(8,128)(2,1)S(1)} %bitcast.7, bf16[64,2048]{1,0:T(8,128)(2,1)S(1)} %reshape.23.refs_1_, bf16[128,2048]{1,0:T(8,128)(2,1)S(1)} %get-tuple-element.10.refs_2_), custom_call_target="tpu_custom_call" | custom-call | flops 1140850688 | bytes 2097152 | tf_op jit(solution)/shard_map/pallas_call | solution.py:193
  43.4 1.9 %collective-permute-start = (f32[32,2048]{1,0:T(8,128)S(1)}, f32[32,2048]{1,0:T(8,128)S(1)}, u32[]{:S(2)}, u32[]{:S(2)}) collective-permute-start(f32[32,2048]{1,0:T(8,128)S(1)} %constant_dynamic-slice_fusion.1), channel_id=1, source_target_pairs={{0,16},{16,0},{32,48},{48,32},{64,80},{80,64},{96,112},{112,96},{1... | collective-permute-start | bytes 786440 | tf_op jit(solution)/shard_map/ppermute | solution.py:213
  45.4 1.5 %collective-permute-done = f32[32,2048]{1,0:T(8,128)S(1)} collective-permute-done((f32[32,2048]{1,0:T(8,128)S(1)}, f32[32,2048]{1,0:T(8,128)S(1)}, u32[]{:S(2)}, u32[]{:S(2)}) %collective-permute-start) | collective-permute-done | bytes 262176 | tf_op jit(solution)/shard_map/ppermute | solution.py:213
  46.9 2.7 %collective-permute-start.1 = (f32[16,2048]{1,0:T(8,128)S(1)}, f32[16,2048]{1,0:T(8,128)S(1)}, u32[]{:S(2)}, u32[]{:S(2)}) collective-permute-start(f32[16,2048]{1,0:T(8,128)S(1)} %constant_dynamic-slice_fusion), channel_id=1, source_target_pairs={{0,256},{16,272},{32,288},{48,304},{64,320},{80,336},{96,352},{112... | collective-permute-start | bytes 393224 | tf_op jit(solution)/shard_map/ppermute | solution.py:213
  49.6 6.2 %collective-permute-done.1 = f32[16,2048]{1,0:T(8,128)S(1)} collective-permute-done((f32[16,2048]{1,0:T(8,128)S(1)}, f32[16,2048]{1,0:T(8,128)S(1)}, u32[]{:S(2)}, u32[]{:S(2)}) %collective-permute-start.1) | collective-permute-done | bytes 131104 | tf_op jit(solution)/shard_map/ppermute | solution.py:213
  55.9 0.7 reshape.25
  56.6 7.1 %all-to-all-start.2 = ((f32[8,2,2048]{2,1,0:T(2,128)}), f32[8,2,2048]{2,1,0:T(2,128)S(1)}, u32[]{:S(2)}, u32[]{:S(2)}) async-start(f32[8,2,2048]{2,1,0:T(2,128)} %reshape.25), calls=%async_computation.2 | async-start | bytes 262144 | tf_op jit(solution)/shard_map/all_to_all | solution.py:216
  63.7 0.9 convert_bitcast_fusion
  64.6 8.2 %all-to-all-done.2 = f32[8,2,2048]{2,1,0:T(2,128)S(1)} async-done(((f32[8,2,2048]{2,1,0:T(2,128)}), f32[8,2,2048]{2,1,0:T(2,128)S(1)}, u32[]{:S(2)}, u32[]{:S(2)}) %all-to-all-start.2) | async-done | bytes 131104 | tf_op jit(solution)/shard_map/all_to_all | solution.py:216
  72.8 3.6 %all-to-all-start.1 = ((f16[16,8,2176]{2,1,0:T(8,128)(2,1)}), f16[16,8,2176]{2,1,0:T(8,128)(2,1)S(1)}, u32[]{:S(2)}, u32[]{:S(2)}) async-start(f16[16,8,2176]{2,1,0:T(8,128)(2,1)} %convert_bitcast_fusion), calls=%async_computation.1 | async-start | bytes 1114112 | tf_op jit(solution)/shard_map/all_to_all | solution.py:189
  76.4 0.7 reduce_sum.9
  77.0 16.2 %all-to-all-done.1 = f16[16,8,2176]{2,1,0:T(8,128)(2,1)S(1)} async-done(((f16[16,8,2176]{2,1,0:T(8,128)(2,1)}), f16[16,8,2176]{2,1,0:T(8,128)(2,1)S(1)}, u32[]{:S(2)}, u32[]{:S(2)}) %all-to-all-start.1) | async-done | bytes 557088 | tf_op jit(solution)/shard_map/all_to_all | solution.py:189
  93.3 1.1 %convert_element_type.7.refs_0_ = f32[16,8,2176]{2,1,0:T(8,128)} convert(f16[16,8,2176]{2,1,0:T(8,128)(2,1)S(1)} %all-to-all-done.1) | non-fusion elementwise | flops 278528 | bytes 1671168 | tf_op jit(solution)/shard_map/convert_element_type | solution.py:229
  94.3 2.5 %shard_map.105 = (f32[8,64]{1,0:T(8,128)}, f32[8,2080]{1,0:T(8,128)}) custom-call(f32[16,8,2176]{2,1,0:T(8,128)} %convert_element_type.7.refs_0_, s32[17,8,128]{2,1,0:T(8,128)} %constant.52.clone.refs_1_, s32[17,8,128]{2,1,0:T(8,128)} %constant.53.clone.refs_2_), custom_call_target="tpu_custom_call" | custom-call | tf_op jit(solution)/shard_map/pallas_call | solution.py:222
  (5 shorter events, 0.1 us)
Async XLA Ops:
  0.6 13.3 %copy-start.1 = (bf16[64,2048]{1,0:T(8,128)(2,1)S(1)}, bf16[64,2048]{1,0:T(8,128)(2,1)}, u32[]{:S(2)}) copy-start(bf16[64,2048]{1,0:T(8,128)(2,1)} %param.11) | copy-start | bytes 786436
  2.7 29.3 %copy-start = (bf16[128,2048]{1,0:T(8,128)(2,1)S(1)}, bf16[128,2048]{1,0:T(8,128)(2,1)}, u32[]{:S(2)}) copy-start(bf16[128,2048]{1,0:T(8,128)(2,1)} %refs_2_.2) | copy-start | bytes 1572868
  2.7 29.3 %all-to-all-start = ((bf16[16,8,2176]{2,1,0:T(8,128)(2,1)}), bf16[16,8,2176]{2,1,0:T(8,128)(2,1)S(1)}, u32[]{:S(2)}, u32[]{:S(2)}) async-start(bf16[16,8,2176]{2,1,0:T(8,128)(2,1)} %shard_map.103), calls=%async_computation | async-start | bytes 1114112 | tf_op jit(solution)/shard_map/all_to_all | solution.py:174
  43.4 3.4 %collective-permute-start = (f32[32,2048]{1,0:T(8,128)S(1)}, f32[32,2048]{1,0:T(8,128)S(1)}, u32[]{:S(2)}, u32[]{:S(2)}) collective-permute-start(f32[32,2048]{1,0:T(8,128)S(1)} %constant_dynamic-slice_fusion.1), channel_id=1, source_target_pairs={{0,16},{16,0},{32,48},{48,32},{64,80},{80,64},{96,112},{112,96},{1... | collective-permute-start | bytes 786440 | tf_op jit(solution)/shard_map/ppermute | solution.py:213
  46.9 8.9 %collective-permute-start.1 = (f32[16,2048]{1,0:T(8,128)S(1)}, f32[16,2048]{1,0:T(8,128)S(1)}, u32[]{:S(2)}, u32[]{:S(2)}) collective-permute-start(f32[16,2048]{1,0:T(8,128)S(1)} %constant_dynamic-slice_fusion), channel_id=1, source_target_pairs={{0,256},{16,272},{32,288},{48,304},{64,320},{80,336},{96,352},{112... | collective-permute-start | bytes 393224 | tf_op jit(solution)/shard_map/ppermute | solution.py:213
  56.6 16.2 %all-to-all-start.2 = ((f32[8,2,2048]{2,1,0:T(2,128)}), f32[8,2,2048]{2,1,0:T(2,128)S(1)}, u32[]{:S(2)}, u32[]{:S(2)}) async-start(f32[8,2,2048]{2,1,0:T(2,128)} %reshape.25), calls=%async_computation.2 | async-start | bytes 262144 | tf_op jit(solution)/shard_map/all_to_all | solution.py:216
  72.8 20.5 %all-to-all-start.1 = ((f16[16,8,2176]{2,1,0:T(8,128)(2,1)}), f16[16,8,2176]{2,1,0:T(8,128)(2,1)S(1)}, u32[]{:S(2)}, u32[]{:S(2)}) async-start(f16[16,8,2176]{2,1,0:T(8,128)(2,1)} %convert_bitcast_fusion), calls=%async_computation.1 | async-start | bytes 1114112 | tf_op jit(solution)/shard_map/all_to_all | solution.py:189

commit v3 on v2

--- a/solution.py
+++ b/solution.py
@@ -32,18 +32,16 @@
     return np.concatenate([source, offset[-1] + order])
 
 
-def gather_tables(source):
-    pad = -len(source) % LANES
-    source = np.concatenate([source, np.full(pad, -1)]).reshape(-1, 1, LANES)
-    source = np.broadcast_to(source, (source.shape[0], 8, LANES)).astype(np.int32)
-    return np.where(source < 0, 0, source % LANES), np.where(source < 0, -1, source // LANES)
-
-
-def permuted(tiles, lane, tile):
+def gather_table(source):
+    return jnp.asarray(np.concatenate([source, np.full(-len(source) % LANES, -1)]).reshape(-1, LANES).astype(np.int32))
+
+
+def permuted(tiles, table_ref, row):
+    source = jnp.broadcast_to(table_ref[row : row + 1], tiles[0].shape)
+    lane, tile = source & (LANES - 1), source >> 7
     total = jnp.zeros(tiles[0].shape, jnp.float32)
     for number, values in enumerate(tiles):
-        moved = jnp.take_along_axis(values, lane, axis=1)
-        total = jnp.where(tile == number, moved, total)
+        total = jnp.where(tile == number, jnp.take_along_axis(values, lane, axis=1), total)
     return total
 
 
@@ -51,14 +49,14 @@
     return [values[:, t : t + LANES] for t in range(0, values.shape[1], LANES)]
 
 
-def spread_kernel(lin_ref, quad_ref, lane_ref, tile_ref, out_ref, wide_ref):
+def spread_kernel(lin_ref, quad_ref, table_ref, out_ref, wide_ref):
     pairs = quad_ref.shape[1]
     wide_ref[...] = jnp.zeros_like(wide_ref)
     wide_ref[:, :pairs] = quad_ref[...].astype(jnp.float32)
     wide_ref[:, pairs : pairs + lin_ref.shape[1]] = lin_ref[...].astype(jnp.float32)
     tiles = tiles_of(wide_ref[...])
-    for t in range(lane_ref.shape[0]):
-        moved = permuted(tiles, lane_ref[t], tile_ref[t]).astype(jnp.bfloat16)
+    for t in range(table_ref.shape[0]):
+        moved = permuted(tiles, table_ref, t).astype(jnp.bfloat16)
         for c in range(out_ref.shape[0]):
             out_ref[c, :, t * LANES : (t + 1) * LANES] = moved
 
@@ -138,15 +136,33 @@
     out_ref[...] = total * scale
 
 
-def gather_kernel(scale, parts_ref, lane_ref, tile_ref, lin_ref, quad_ref, wide_ref):
+def pack_kernel(kept_ref, came_ref, out_ref):
+    columns = kept_ref.shape[1]
+    total = kept_ref[...] + came_ref[...]
+    top = jnp.max(jnp.max(jnp.abs(total), axis=0, keepdims=True), axis=1, keepdims=True)
+    level = jnp.floor(jnp.log2(jnp.maximum(top, 2.0**-100)))
+    out_ref[:, :columns] = total * jnp.exp2(TOP - level)
+    out_ref[:, columns:] = jnp.broadcast_to(level, (total.shape[0], LANES))
+
+
+def unpack_kernel(parts_ref, out_ref):
+    columns = out_ref.shape[1]
+    total = jnp.zeros(out_ref.shape, jnp.float32)
+    for p in range(parts_ref.shape[0]):
+        part = parts_ref[p]
+        total = total + part[:, :columns] * jnp.exp2(part[:, columns : columns + 1] - TOP)
+    out_ref[...] = total
+
+
+def gather_kernel(scale, parts_ref, table_ref, lin_ref, quad_ref, wide_ref):
     pairs = quad_ref.shape[1]
     total = jnp.zeros(parts_ref.shape[1:], jnp.float32)
     for p in range(parts_ref.shape[0]):
         part = parts_ref[p]
         total = total + part * jnp.exp2(part[:, pairs : pairs + 1] - TOP)
     tiles = tiles_of(total * scale)
-    for t in range(lane_ref.shape[0]):
-        wide_ref[:, t * LANES : (t + 1) * LANES] = permuted(tiles, lane_ref[t], tile_ref[t])
+    for t in range(table_ref.shape[0]):
+        wide_ref[:, t * LANES : (t + 1) * LANES] = permuted(tiles, table_ref, t)
     quad_ref[...] = wide_ref[:, :pairs]
     lin_ref[...] = wide_ref[:, pairs : pairs + lin_ref.shape[1]]
 
@@ -161,19 +177,18 @@
     source = column_source(count)
     width = len(source)
     padded = pairs + count + -(pairs + count) % LANES
-    lane, tile = gather_tables(source)
     back_source = np.zeros(pairs + count, np.int64)
     back_source[source[source >= 0]] = np.nonzero(source >= 0)[0]
-    back_lane, back_tile = gather_tables(back_source)
 
     own = pl.pallas_call(
         spread_kernel,
         out_shape=jax.ShapeDtypeStruct((snap_parts, own_rows, width), jnp.bfloat16),
         scratch_shapes=[pltpu.VMEM((own_rows, padded), jnp.float32)],
-    )(linear_basis, quad_weights, jnp.asarray(lane), jnp.asarray(tile))
+    )(linear_basis, quad_weights, gather_table(source))
     maps = lax.all_to_all(own, "snaps", 0, 0, tiled=True).reshape(local_rows, width)
     coords = coordinates.reshape(FAR, RING, CORES, -1, snap_dev).transpose(2, 0, 1, 3, 4).reshape(count, snap_dev)
 
+    block = min(BLOCK, snap_dev)
     flops = 2 * local_rows * width * snap_dev
     grad, residual = pl.pallas_call(
         lambda *refs: forward_kernel(pairs, *refs),
@@ -188,7 +203,6 @@
     grad = grad.astype(jnp.float16).reshape(snap_parts, own_rows, width)
     grad_parts = lax.all_to_all(grad, "snaps", 0, 0, tiled=True)
 
-    block = min(BLOCK, snap_dev)
     coord_scale = 1.0 / math.sqrt(local_rows * row_parts)
     coord_part = pl.pallas_call(
         lambda *refs: backward_kernel(coord_scale, *refs),
@@ -206,17 +220,24 @@
     )(maps, coords, residual)
 
     place = lax.axis_index("rows")
-    for apart, own_half in ((1, place % CORES), (CORES * RING, place // (CORES * RING))):
-        half = coord_part.shape[0] // 2
-        sent = lax.dynamic_slice_in_dim(coord_part, (1 - own_half) * half, half, 0)
-        kept = lax.dynamic_slice_in_dim(coord_part, own_half * half, half, 0)
-        came = lax.ppermute(sent, "rows", [(i, i ^ apart) for i in range(row_parts)])
-        coord_part = kept + came
-    rings = [[(f * RING + y) * CORES + c for y in range(RING)] for f in range(FAR) for c in range(CORES)]
-    coord_parts = lax.all_to_all(
-        coord_part.reshape(RING, -1, snap_dev), "rows", 0, 0, axis_index_groups=rings, tiled=True
-    )
-    grad_coords = jnp.sum(coord_parts, axis=0)
+    half = count // CORES
+    core = place % CORES
+    sent = lax.dynamic_slice_in_dim(coord_part, (1 - core) * half, half, 0)
+    kept = lax.dynamic_slice_in_dim(coord_part, core * half, half, 0)
+    came = lax.ppermute(sent, "rows", [(i, i ^ 1) for i in range(row_parts)])
+    chips = [list(range(first, row_parts, CORES)) for first in range(CORES)]
+    packed = pl.pallas_call(
+        pack_kernel,
+        out_shape=jax.ShapeDtypeStruct((half, snap_dev + LANES), jnp.float32),
+        compiler_params=pltpu.CompilerParams(vmem_limit_bytes=4 << 20),
+    )(kept, came)
+    packed = packed.astype(jnp.float16).reshape(FAR * RING, -1, snap_dev + LANES)
+    coord_parts = lax.all_to_all(packed, "rows", 0, 0, axis_index_groups=chips, tiled=True)
+    grad_coords = pl.pallas_call(
+        unpack_kernel,
+        out_shape=jax.ShapeDtypeStruct((coord_parts.shape[1], snap_dev), jnp.float32),
+        compiler_params=pltpu.CompilerParams(vmem_limit_bytes=4 << 20),
+    )(coord_parts.astype(jnp.float32))
 
     model_scale = 1.0 / math.sqrt(snap_dev * snap_parts)
     grad_basis, grad_quad = pl.pallas_call(
@@ -226,7 +247,7 @@
             jax.ShapeDtypeStruct(quad_weights.shape, jnp.float32),
         ],
         scratch_shapes=[pltpu.VMEM((own_rows, padded), jnp.float32)],
-    )(grad_parts.astype(jnp.float32), jnp.asarray(back_lane), jnp.asarray(back_tile))
+    )(grad_parts.astype(jnp.float32), gather_table(back_source))
     return (grad_basis, grad_quad, grad_coords)
 
 

time: 97.3 us -> 92.7 us (0.953)
  the two profiles are of different devices: /device:TPU:4 before, /device:TPU:8 now
where the time goes in v3:
time: 92.7 us; the launch traced here: 92.3 us
  waiting for transfers between devices  45 us (49%)
  starting transfers between devices  26.7 us (29%)
  Pallas kernels  16.5 us (18%)
  other arithmetic  2.05 us (2%)
  local copies, waits for them, and re-layouts  1.25 us (1%)
    all_to_all x1, waiting for transfers between devices, shards(): lax.all_to_all(own, 'snaps', 0, 0, tiled=True).reshape(local_rows, width)  17.6 us
    all_to_all x1, waiting for transfers between devices, shards(): grad_parts = lax.all_to_all(grad, 'snaps', 0, 0, tiled=True)  16.8 us
    all_to_all x1, starting transfers between devices, shards(): lax.all_to_all(own, 'snaps', 0, 0, tiled=True).reshape(local_rows, width)  11.5 us
    all_to_all x1, starting transfers between devices, shards(): lax.all_to_all(packed, 'rows', 0, 0, axis_index_groups=chips, tiled=True)  9.73 us
    all_to_all x1, waiting for transfers between devices, shards(): lax.all_to_all(packed, 'rows', 0, 0, axis_index_groups=chips, tiled=True)  9.11 us
    pallas_call x1, Pallas kernels, shards(): pl.pallas_call(lambda *refs: forward_kernel(pairs, *refs), out_shape=[jax...  6.25 us
    pallas_call x1, Pallas kernels, shards(): pl.pallas_call(lambda *refs: backward_kernel(coord_scale, *refs), grid=(s...  5.06 us
    all_to_all x1, starting transfers between devices, shards(): grad_parts = lax.all_to_all(grad, 'snaps', 0, 0, tiled=True)  3.58 us
  transfers between devices with their start and end apart: 4, of which 4 were waited for; matrix products, arithmetic and copies ran while one was open for 2% of the time, Pallas kernels for 1%

profile of v3, /device:TPU:8, one launch (start us, length us, event | category | flops | bytes accessed | tf_op | source)
XLA Modules:
  0.0 92.3 jit_solution(7934345251245660911)
XLA Ops:
  0.6 0.0 copy-start.1
  0.6 1.9 %shard_map.85 = bf16[16,8,2176]{2,1,0:T(8,128)(2,1)} custom-call(bf16[8,64]{1,0:T(8,128)(2,1)} %lin_ref.1, bf16[8,2080]{1,0:T(8,128)(2,1)} %quad_ref.1, s32[17,128]{1,0:T(8,128)} %constant.29.clone.table_ref), custom_call_target="tpu_custom_call" | custom-call | tf_op jit(solution)/shard_map/pallas_call | solution.py:183
  2.6 11.5 %all-to-all-start = ((bf16[16,8,2176]{2,1,0:T(8,128)(2,1)}), bf16[16,8,2176]{2,1,0:T(8,128)(2,1)S(1)}, u32[]{:S(2)}, u32[]{:S(2)}) async-start(bf16[16,8,2176]{2,1,0:T(8,128)(2,1)} %shard_map.85), calls=%async_computation | async-start | bytes 1114112 | tf_op jit(solution)/shard_map/all_to_all | solution.py:188
  14.1 0.0 copy-done.1
  14.1 0.2 reshape.22
  14.3 0.2 copy.11
  14.5 0.1 reshape.23.refs_1_
  14.6 17.6 %all-to-all-done = bf16[16,8,2176]{2,1,0:T(8,128)(2,1)S(1)} async-done(((bf16[16,8,2176]{2,1,0:T(8,128)(2,1)}), bf16[16,8,2176]{2,1,0:T(8,128)(2,1)S(1)}, u32[]{:S(2)}, u32[]{:S(2)}) %all-to-all-start) | async-done | bytes 557088 | tf_op jit(solution)/shard_map/all_to_all | solution.py:188
  32.2 0.0 copy-done
  32.2 6.3 %shard_map.86 = (f32[128,2176]{1,0:T(8,128)S(1)}, bf16[128,2048]{1,0:T(8,128)(2,1)S(1)}) custom-call(bf16[128,2176]{1,0:T(8,128)(2,1)S(1)} %bitcast.6, bf16[64,2048]{1,0:T(8,128)(2,1)S(1)} %reshape.23.refs_1_, bf16[128,2048]{1,0:T(8,128)(2,1)S(1)} %copy-done), custom_call_target="tpu_custom_call" | custom-call | flops 2281701376 | bytes 4194304 | tf_op jit(solution)/shard_map/pallas_call | solution.py:193
  38.4 5.1 %shard_map.88 = f32[64,2048]{1,0:T(8,128)S(1)} custom-call(bf16[128,2176]{1,0:T(8,128)(2,1)S(1)} %bitcast.7, bf16[64,2048]{1,0:T(8,128)(2,1)S(1)} %reshape.23.refs_1_, bf16[128,2048]{1,0:T(8,128)(2,1)S(1)} %get-tuple-element.10.refs_2_), custom_call_target="tpu_custom_call" | custom-call | flops 1140850688 | bytes 2097152 | tf_op jit(solution)/shard_map/pallas_call | solution.py:207
  43.6 1.9 %collective-permute-start = (f32[32,2048]{1,0:T(8,128)S(1)}, f32[32,2048]{1,0:T(8,128)S(1)}, u32[]{:S(2)}, u32[]{:S(2)}) collective-permute-start(f32[32,2048]{1,0:T(8,128)S(1)} %get-tuple-element.11), channel_id=1, source_target_pairs={{0,16},{16,0},{32,48},{48,32},{64,80},{80,64},{96,112},{112,96},{1... | collective-permute-start | bytes 786440 | tf_op jit(solution)/shard_map/ppermute | solution.py:227
  45.5 1.5 %collective-permute-done.came_ref = f32[32,2048]{1,0:T(8,128)S(1)} collective-permute-done((f32[32,2048]{1,0:T(8,128)S(1)}, f32[32,2048]{1,0:T(8,128)S(1)}, u32[]{:S(2)}, u32[]{:S(2)}) %collective-permute-start) | collective-permute-done | bytes 262176 | tf_op jit(solution)/shard_map/ppermute | solution.py:227
  47.0 0.1 shard_map.89
  47.2 0.7 reshape.25
  47.9 9.7 %all-to-all-start.2 = ((f16[16,2,2176]{2,1,0:T(2,128)(2,1)}), f16[16,2,2176]{2,1,0:T(2,128)(2,1)S(1)}, u32[]{:S(2)}, u32[]{:S(2)}) async-start(f16[16,2,2176]{2,1,0:T(2,128)(2,1)} %reshape.25), calls=%async_computation.2 | async-start | bytes 278528 | tf_op jit(solution)/shard_map/all_to_all | solution.py:235
  57.6 0.9 convert_bitcast_fusion
  58.5 9.1 %all-to-all-done.2 = f16[16,2,2176]{2,1,0:T(2,128)(2,1)S(1)} async-done(((f16[16,2,2176]{2,1,0:T(2,128)(2,1)}), f16[16,2,2176]{2,1,0:T(2,128)(2,1)S(1)}, u32[]{:S(2)}, u32[]{:S(2)}) %all-to-all-start.2) | async-done | bytes 139296 | tf_op jit(solution)/shard_map/all_to_all | solution.py:235
  67.6 3.6 %all-to-all-start.1 = ((f16[16,8,2176]{2,1,0:T(8,128)(2,1)}), f16[16,8,2176]{2,1,0:T(8,128)(2,1)S(1)}, u32[]{:S(2)}, u32[]{:S(2)}) async-start(f16[16,8,2176]{2,1,0:T(8,128)(2,1)} %convert_bitcast_fusion), calls=%async_computation.1 | async-start | bytes 1114112 | tf_op jit(solution)/shard_map/all_to_all | solution.py:204
  71.2 0.1 convert_element_type.15.parts_ref
  71.3 0.7 shard_map.90
  72.0 16.8 %all-to-all-done.1 = f16[16,8,2176]{2,1,0:T(8,128)(2,1)S(1)} async-done(((f16[16,8,2176]{2,1,0:T(8,128)(2,1)}), f16[16,8,2176]{2,1,0:T(8,128)(2,1)S(1)}, u32[]{:S(2)}, u32[]{:S(2)}) %all-to-all-start.1) | async-done | bytes 557088 | tf_op jit(solution)/shard_map/all_to_all | solution.py:204
  88.8 1.1 %convert_element_type.13.refs_0_ = f32[16,8,2176]{2,1,0:T(8,128)} convert(f16[16,8,2176]{2,1,0:T(8,128)(2,1)S(1)} %all-to-all-done.1) | non-fusion elementwise | flops 278528 | bytes 1671168 | tf_op jit(solution)/shard_map/convert_element_type | solution.py:250
  89.8 2.5 %shard_map.87 = (f32[8,64]{1,0:T(8,128)}, f32[8,2080]{1,0:T(8,128)}) custom-call(f32[16,8,2176]{2,1,0:T(8,128)} %convert_element_type.13.refs_0_, s32[17,128]{1,0:T(8,128)} %constant.30.clone.refs_1_), custom_call_target="tpu_custom_call" | custom-call | tf_op jit(solution)/shard_map/pallas_call | solution.py:243
  (3 shorter events, 0.1 us)
Async XLA Ops:
  0.6 13.4 %copy-start.1 = (bf16[64,2048]{1,0:T(8,128)(2,1)S(1)}, bf16[64,2048]{1,0:T(8,128)(2,1)}, u32[]{:S(2)}) copy-start(bf16[64,2048]{1,0:T(8,128)(2,1)} %param.9) | copy-start | bytes 786436
  2.6 29.6 %copy-start = (bf16[128,2048]{1,0:T(8,128)(2,1)S(1)}, bf16[128,2048]{1,0:T(8,128)(2,1)}, u32[]{:S(2)}) copy-start(bf16[128,2048]{1,0:T(8,128)(2,1)} %refs_2_.1) | copy-start | bytes 1572868
  2.6 29.6 %all-to-all-start = ((bf16[16,8,2176]{2,1,0:T(8,128)(2,1)}), bf16[16,8,2176]{2,1,0:T(8,128)(2,1)S(1)}, u32[]{:S(2)}, u32[]{:S(2)}) async-start(bf16[16,8,2176]{2,1,0:T(8,128)(2,1)} %shard_map.85), calls=%async_computation | async-start | bytes 1114112 | tf_op jit(solution)/shard_map/all_to_all | solution.py:188
  43.6 3.4 %collective-permute-start = (f32[32,2048]{1,0:T(8,128)S(1)}, f32[32,2048]{1,0:T(8,128)S(1)}, u32[]{:S(2)}, u32[]{:S(2)}) collective-permute-start(f32[32,2048]{1,0:T(8,128)S(1)} %get-tuple-element.11), channel_id=1, source_target_pairs={{0,16},{16,0},{32,48},{48,32},{64,80},{80,64},{96,112},{112,96},{1... | collective-permute-start | bytes 786440 | tf_op jit(solution)/shard_map/ppermute | solution.py:227
  47.9 19.7 %all-to-all-start.2 = ((f16[16,2,2176]{2,1,0:T(2,128)(2,1)}), f16[16,2,2176]{2,1,0:T(2,128)(2,1)S(1)}, u32[]{:S(2)}, u32[]{:S(2)}) async-start(f16[16,2,2176]{2,1,0:T(2,128)(2,1)} %reshape.25), calls=%async_computation.2 | async-start | bytes 278528 | tf_op jit(solution)/shard_map/all_to_all | solution.py:235
  67.6 21.2 %all-to-all-start.1 = ((f16[16,8,2176]{2,1,0:T(8,128)(2,1)}), f16[16,8,2176]{2,1,0:T(8,128)(2,1)S(1)}, u32[]{:S(2)}, u32[]{:S(2)}) async-start(f16[16,8,2176]{2,1,0:T(8,128)(2,1)} %convert_bitcast_fusion), calls=%async_computation.1 | async-start | bytes 1114112 | tf_op jit(solution)/shard_map/all_to_all | solution.py:204

commit v4 on v3

--- a/solution.py
+++ b/solution.py
@@ -185,7 +185,15 @@
         out_shape=jax.ShapeDtypeStruct((snap_parts, own_rows, width), jnp.bfloat16),
         scratch_shapes=[pltpu.VMEM((own_rows, padded), jnp.float32)],
     )(linear_basis, quad_weights, gather_table(source))
-    maps = lax.all_to_all(own, "snaps", 0, 0, tiled=True).reshape(local_rows, width)
+    place = lax.axis_index("rows")
+    core = place % CORES
+    both = ("rows", "snaps")
+    spread = [int(f"{z:04b}"[::-1], 2) for z in range(snap_parts)]
+    lines = [[r * snap_parts + z for z in spread][:: 1 - 2 * (r % CORES)] for r in range(row_parts)]
+    maps = lax.all_to_all(own, both, 0, 0, axis_index_groups=lines, tiled=True).reshape(local_rows, width)
+    stacked = snapshots.reshape(2, 2, 2, 2, own_rows, snap_dev).transpose(3, 2, 1, 0, 4, 5)
+    stacked = stacked.reshape(snap_parts, own_rows, snap_dev)
+    snapshots = jnp.where(core == 1, stacked[::-1], stacked).reshape(local_rows, snap_dev)
     coords = coordinates.reshape(FAR, RING, CORES, -1, snap_dev).transpose(2, 0, 1, 3, 4).reshape(count, snap_dev)
 
     block = min(BLOCK, snap_dev)
@@ -201,7 +209,7 @@
         cost_estimate=pl.CostEstimate(flops=2 * flops, bytes_accessed=4 << 20, transcendentals=0),
     )(maps, coords, snapshots)
     grad = grad.astype(jnp.float16).reshape(snap_parts, own_rows, width)
-    grad_parts = lax.all_to_all(grad, "snaps", 0, 0, tiled=True)
+    grad_parts = lax.all_to_all(grad, both, 0, 0, axis_index_groups=lines, tiled=True)
 
     coord_scale = 1.0 / math.sqrt(local_rows * row_parts)
     coord_part = pl.pallas_call(
@@ -219,19 +227,18 @@
         cost_estimate=pl.CostEstimate(flops=flops, bytes_accessed=2 << 20, transcendentals=0),
     )(maps, coords, residual)
 
-    place = lax.axis_index("rows")
     half = count // CORES
-    core = place % CORES
     sent = lax.dynamic_slice_in_dim(coord_part, (1 - core) * half, half, 0)
     kept = lax.dynamic_slice_in_dim(coord_part, core * half, half, 0)
     came = lax.ppermute(sent, "rows", [(i, i ^ 1) for i in range(row_parts)])
-    chips = [list(range(first, row_parts, CORES)) for first in range(CORES)]
+    chips = [list(range(first, row_parts, CORES))[:: 1 - 2 * first] for first in range(CORES)]
     packed = pl.pallas_call(
         pack_kernel,
         out_shape=jax.ShapeDtypeStruct((half, snap_dev + LANES), jnp.float32),
         compiler_params=pltpu.CompilerParams(vmem_limit_bytes=4 << 20),
     )(kept, came)
     packed = packed.astype(jnp.float16).reshape(FAR * RING, -1, snap_dev + LANES)
+    packed = jnp.where(core == 1, packed[::-1], packed)
     coord_parts = lax.all_to_all(packed, "rows", 0, 0, axis_index_groups=chips, tiled=True)
     grad_coords = pl.pallas_call(
         unpack_kernel,

time: 92.7 us -> 88.9 us (0.959)
  the two profiles are of different devices: /device:TPU:8 before, /device:TPU:6 now
where the time goes in v4:
time: 88.9 us; the launch traced here: 88.5 us
  waiting for transfers between devices  37.6 us (42%)
  starting transfers between devices  29.9 us (34%)
  Pallas kernels  16.6 us (19%)
  other arithmetic  2.96 us (3%)
    all_to_all x1, waiting for transfers between devices, shards(): lax.all_to_all(own, both, 0, 0, axis_index_groups=lines, tiled=True)  15.2 us
    all_to_all x1, waiting for transfers between devices, shards(): lax.all_to_all(grad, both, 0, 0, axis_index_groups=lines, tiled=True)  14.3 us
    all_to_all x1, starting transfers between devices, shards(): lax.all_to_all(own, both, 0, 0, axis_index_groups=lines, tiled=True)  11.9 us
    all_to_all x1, starting transfers between devices, shards(): lax.all_to_all(packed, 'rows', 0, 0, axis_index_groups=chips, tiled=True)  10.1 us
    all_to_all x1, waiting for transfers between devices, shards(): lax.all_to_all(packed, 'rows', 0, 0, axis_index_groups=chips, tiled=True)  6.71 us
    pallas_call x1, Pallas kernels, shards(): pl.pallas_call(lambda *refs: forward_kernel(pairs, *refs), out_shape=[jax...  6.28 us
    all_to_all x1, starting transfers between devices, shards(): lax.all_to_all(grad, both, 0, 0, axis_index_groups=lines, tiled=True)  5.98 us
    pallas_call x1, Pallas kernels, shards(): pl.pallas_call(lambda *refs: backward_kernel(coord_scale, *refs), grid=(s...  5.06 us
  transfers between devices with their start and end apart: 4, of which 4 were waited for; matrix products, arithmetic and copies ran while one was open for 2% of the time, Pallas kernels for 1%

profile of v4, /device:TPU:6, one launch (start us, length us, event | category | flops | bytes accessed | tf_op | source)
XLA Modules:
  0.0 88.5 jit_solution(2082380646541270469)
XLA Ops:
  0.6 0.0 copy-start
  0.6 1.9 %shard_map.85 = bf16[16,8,2176]{2,1,0:T(8,128)(2,1)} custom-call(bf16[8,64]{1,0:T(8,128)(2,1)} %lin_ref.1, bf16[8,2080]{1,0:T(8,128)(2,1)} %quad_ref.1, s32[17,128]{1,0:T(8,128)} %constant.29.clone.table_ref), custom_call_target="tpu_custom_call" | custom-call | tf_op jit(solution)/shard_map/pallas_call | solution.py:183
  2.6 11.9 %all-to-all-start = ((bf16[16,8,2176]{2,1,0:T(8,128)(2,1)}), bf16[16,8,2176]{2,1,0:T(8,128)(2,1)S(1)}, u32[]{:S(2)}, u32[]{:S(2)}) async-start(bf16[16,8,2176]{2,1,0:T(8,128)(2,1)} %shard_map.85), calls=%async_computation | async-start | bytes 1114112 | tf_op jit(solution)/shard_map/all_to_all | solution.py:193
  14.6 0.2 reshape.31
  14.8 0.2 copy.12
  15.0 0.1 reshape.32.refs_1_
  15.1 0.1 fusion.refs_2_
  15.2 15.2 %all-to-all-done = bf16[16,8,2176]{2,1,0:T(8,128)(2,1)S(1)} async-done(((bf16[16,8,2176]{2,1,0:T(8,128)(2,1)}), bf16[16,8,2176]{2,1,0:T(8,128)(2,1)S(1)}, u32[]{:S(2)}, u32[]{:S(2)}) %all-to-all-start) | async-done | bytes 557088 | tf_op jit(solution)/shard_map/all_to_all | solution.py:193
  30.3 6.3 %shard_map.86 = (f32[128,2176]{1,0:T(8,128)S(1)}, bf16[128,2048]{1,0:T(8,128)(2,1)S(1)}) custom-call(bf16[128,2176]{1,0:T(8,128)(2,1)S(1)} %bitcast.12, bf16[64,2048]{1,0:T(8,128)(2,1)S(1)} %reshape.32.refs_1_, bf16[128,2048]{1,0:T(8,128)(2,1)S(1)} %fusion.refs_2_), custom_call_target="tpu_custom_call" | custom-call | flops 2281701376 | bytes 4194304 | tf_op jit(solution)/shard_map/pallas_call | solution.py:201
  36.6 5.1 %shard_map.88 = f32[64,2048]{1,0:T(8,128)S(1)} custom-call(bf16[128,2176]{1,0:T(8,128)(2,1)S(1)} %bitcast.13, bf16[64,2048]{1,0:T(8,128)(2,1)S(1)} %reshape.32.refs_1_, bf16[128,2048]{1,0:T(8,128)(2,1)S(1)} %get-tuple-element.10.refs_2_), custom_call_target="tpu_custom_call" | custom-call | flops 1140850688 | bytes 2097152 | tf_op jit(solution)/shard_map/pallas_call | solution.py:215
  41.8 1.9 %collective-permute-start = (f32[32,2048]{1,0:T(8,128)S(1)}, f32[32,2048]{1,0:T(8,128)S(1)}, u32[]{:S(2)}, u32[]{:S(2)}) collective-permute-start(f32[32,2048]{1,0:T(8,128)S(1)} %get-tuple-element.11), channel_id=1, source_target_pairs={{0,16},{16,0},{32,48},{48,32},{64,80},{80,64},{96,112},{112,96},{1... | collective-permute-start | bytes 786440 | tf_op jit(solution)/shard_map/ppermute | solution.py:233
  43.7 1.5 %collective-permute-done.came_ref = f32[32,2048]{1,0:T(8,128)S(1)} collective-permute-done((f32[32,2048]{1,0:T(8,128)S(1)}, f32[32,2048]{1,0:T(8,128)S(1)}, u32[]{:S(2)}, u32[]{:S(2)}) %collective-permute-start) | collective-permute-done | bytes 262176 | tf_op jit(solution)/shard_map/ppermute | solution.py:233
  45.2 0.1 shard_map.89
  45.4 0.1 reshape.37
  45.4 0.8 broadcast_select_fusion
  46.2 10.1 %all-to-all-start.2 = ((f16[16,2,2176]{2,1,0:T(2,128)(2,1)}), f16[16,2,2176]{2,1,0:T(2,128)(2,1)S(1)}, u32[]{:S(2)}, u32[]{:S(2)}) async-start(f16[16,2,2176]{2,1,0:T(2,128)(2,1)} %broadcast_select_fusion), calls=%async_computation.2 | async-start | bytes 278528 | tf_op jit(solution)/shard_map/all_to_all | solution.py:242
  56.3 0.9 convert_bitcast_fusion
  57.2 6.7 %all-to-all-done.2 = f16[16,2,2176]{2,1,0:T(2,128)(2,1)S(1)} async-done(((f16[16,2,2176]{2,1,0:T(2,128)(2,1)}), f16[16,2,2176]{2,1,0:T(2,128)(2,1)S(1)}, u32[]{:S(2)}, u32[]{:S(2)}) %all-to-all-start.2) | async-done | bytes 139296 | tf_op jit(solution)/shard_map/all_to_all | solution.py:242
  63.9 6.0 %all-to-all-start.1 = ((f16[16,8,2176]{2,1,0:T(8,128)(2,1)}), f16[16,8,2176]{2,1,0:T(8,128)(2,1)S(1)}, u32[]{:S(2)}, u32[]{:S(2)}) async-start(f16[16,8,2176]{2,1,0:T(8,128)(2,1)} %convert_bitcast_fusion), calls=%async_computation.1 | async-start | bytes 1114112 | tf_op jit(solution)/shard_map/all_to_all | solution.py:212
  69.9 0.1 convert_element_type.15.parts_ref
  70.0 0.7 shard_map.90
  70.7 14.3 %all-to-all-done.1 = f16[16,8,2176]{2,1,0:T(8,128)(2,1)S(1)} async-done(((f16[16,8,2176]{2,1,0:T(8,128)(2,1)}), f16[16,8,2176]{2,1,0:T(8,128)(2,1)S(1)}, u32[]{:S(2)}, u32[]{:S(2)}) %all-to-all-start.1) | async-done | bytes 557088 | tf_op jit(solution)/shard_map/all_to_all | solution.py:212
  84.9 1.1 %convert_element_type.13.refs_0_ = f32[16,8,2176]{2,1,0:T(8,128)} convert(f16[16,8,2176]{2,1,0:T(8,128)(2,1)S(1)} %all-to-all-done.1) | non-fusion elementwise | flops 278528 | bytes 1671168 | tf_op jit(solution)/shard_map/convert_element_type | solution.py:257
  86.0 2.5 %shard_map.87 = (f32[8,64]{1,0:T(8,128)}, f32[8,2080]{1,0:T(8,128)}) custom-call(f32[16,8,2176]{2,1,0:T(8,128)} %convert_element_type.13.refs_0_, s32[17,128]{1,0:T(8,128)} %constant.30.clone.refs_1_), custom_call_target="tpu_custom_call" | custom-call | tf_op jit(solution)/shard_map/pallas_call | solution.py:250
  (6 shorter events, 0.1 us)
Async XLA Ops:
  0.6 13.9 %copy-start = (bf16[128,2048]{1,0:T(8,128)(2,1)S(1)}, bf16[128,2048]{1,0:T(8,128)(2,1)}, u32[]{:S(2)}) copy-start(bf16[128,2048]{1,0:T(8,128)(2,1)} %param.6) | copy-start | bytes 1572868
  2.6 12.0 %copy-start.1 = (bf16[64,2048]{1,0:T(8,128)(2,1)S(1)}, bf16[64,2048]{1,0:T(8,128)(2,1)}, u32[]{:S(2)}) copy-start(bf16[64,2048]{1,0:T(8,128)(2,1)} %param.9) | copy-start | bytes 786436
  2.6 27.8 %all-to-all-start = ((bf16[16,8,2176]{2,1,0:T(8,128)(2,1)}), bf16[16,8,2176]{2,1,0:T(8,128)(2,1)S(1)}, u32[]{:S(2)}, u32[]{:S(2)}) async-start(bf16[16,8,2176]{2,1,0:T(8,128)(2,1)} %shard_map.85), calls=%async_computation | async-start | bytes 1114112 | tf_op jit(solution)/shard_map/all_to_all | solution.py:193
  41.8 3.4 %collective-permute-start = (f32[32,2048]{1,0:T(8,128)S(1)}, f32[32,2048]{1,0:T(8,128)S(1)}, u32[]{:S(2)}, u32[]{:S(2)}) collective-permute-start(f32[32,2048]{1,0:T(8,128)S(1)} %get-tuple-element.11), channel_id=1, source_target_pairs={{0,16},{16,0},{32,48},{48,32},{64,80},{80,64},{96,112},{112,96},{1... | collective-permute-start | bytes 786440 | tf_op jit(solution)/shard_map/ppermute | solution.py:233
  46.2 17.7 %all-to-all-start.2 = ((f16[16,2,2176]{2,1,0:T(2,128)(2,1)}), f16[16,2,2176]{2,1,0:T(2,128)(2,1)S(1)}, u32[]{:S(2)}, u32[]{:S(2)}) async-start(f16[16,2,2176]{2,1,0:T(2,128)(2,1)} %broadcast_select_fusion), calls=%async_computation.2 | async-start | bytes 278528 | tf_op jit(solution)/shard_map/all_to_all | solution.py:242
  63.9 21.0 %all-to-all-start.1 = ((f16[16,8,2176]{2,1,0:T(8,128)(2,1)}), f16[16,8,2176]{2,1,0:T(8,128)(2,1)S(1)}, u32[]{:S(2)}, u32[]{:S(2)}) async-start(f16[16,8,2176]{2,1,0:T(8,128)(2,1)} %convert_bitcast_fusion), calls=%async_computation.1 | async-start | bytes 1114112 | tf_op jit(solution)/shard_map/all_to_all | solution.py:212
